TPU v7x, 128 devices: a whole 4x4x4 slice. The times are simulated.
128 devices in a mesh: expert: 8 (over z_lo, x), shard: 16 (over z_hi, y, core).
Axes of the slice: x: 4, y: 4, z: 4 (z_hi: 2, z_lo: 2; z = z_hi * 2 + z_lo), core: 2. Of those that a mesh axis runs over, the one named last changes fastest.
Arguments:
- grad_out: bfloat16 [8, 2048, 3072], P('expert', 'shard'), may hold values from -6 to 6
- gate_pre: bfloat16 [8, 2048, 8192], P('expert', None, 'shard'), may hold values from -8 to 8
- up_pre: bfloat16 [8, 2048, 8192], P('expert', None, 'shard'), may hold values from -6 to 6
- counts: int32 [8, 16], P('expert', 'shard'), may hold values from 32 to 128
- placement: int32 [8], replicated, may hold values from 0 to 63, as said below
- master: float32 [8, 8192, 3072], P('expert', 'shard')
Outputs:
- d_gate: bfloat16 [8, 2048, 8192], P('expert', None, 'shard')
- d_up: bfloat16 [8, 2048, 8192], P('expert', None, 'shard')
- new_master: float32 [8, 8192, 3072], P('expert', 'shard')
Inputs may be any that keep to these rules, and one draw needn't show every extreme that they name: `placement`: slots that hold the same expert form aligned blocks of 1, 2 or 4 consecutive slots, each block starting at a multiple of its size; different blocks hold different experts.
All inputs are finite; a program needn't handle non-finite values.
Results may differ from a plain program's by a relative error of at most 0.006.
Values may be sent and summed in bfloat16 or wider, within the bound.
A program may use at most 256 MiB of HBM per device.

v0:
```python
import jax
import jax.numpy as jnp
from jax import lax
from jax.sharding import PartitionSpec as P

learn_rate = 0.02
rms_eps = 1e-06


def from_partner(shard, axis, bit):
    return lax.ppermute(shard, axis, [(i, i ^ 1 << bit) for i in range(lax.axis_size(axis))])


def per_device(grad_out, gate_pre, up_pre, counts, placement, master):
    weight_work = master[0].astype(jnp.bfloat16)
    local_rows = grad_out.shape[1]
    row_valid = (jnp.arange(local_rows, dtype=jnp.int32) < counts[0, 0]).astype(jnp.bfloat16)
    masked = grad_out[0] * row_valid[:, None]
    gate_val = gate_pre[0].astype(jnp.float32)
    up_val = up_pre[0].astype(jnp.float32)
    gate_sig = jax.nn.sigmoid(gate_val)
    gate_act = gate_val * gate_sig
    gate_slope = gate_sig * (1.0 + gate_val * (1.0 - gate_sig))
    hidden = (gate_act * up_val).astype(jnp.bfloat16)
    my_slot = lax.axis_index("expert")
    slot_order = jnp.arange(placement.shape[0], dtype=jnp.int32)
    my_expert = jnp.sum(jnp.where(slot_order == my_slot, placement, 0))
    block_rows = lax.all_gather(masked, "shard", axis=0, tiled=True)
    d_hidden = lax.dot_general(
        block_rows, weight_work, (((1,), (1,)), ((), ())), preferred_element_type=jnp.float32
    )
    up_acc = (d_hidden * gate_act).astype(jnp.bfloat16)
    gate_acc = (d_hidden * up_val * gate_slope).astype(jnp.bfloat16)
    grad_acc = lax.dot_general(
        hidden, block_rows, (((0,), (0,)), ((), ())), preferred_element_type=jnp.float32
    )
    grad_sum = grad_acc
    for bit_pos in range(2):
        received = from_partner(grad_sum.astype(jnp.bfloat16), "expert", bit_pos).astype(
            grad_sum.dtype
        )
        other_slot = jnp.bitwise_xor(my_slot, 1 << bit_pos)
        their_expert = jnp.sum(jnp.where(slot_order == other_slot, placement, 0))
        grad_sum = grad_sum + jnp.where(my_expert == their_expert, received, 0.0)
    row_rms = jnp.sqrt(jnp.mean(grad_sum * grad_sum, axis=1, keepdims=True) + rms_eps)
    new_master = master[0] - learn_rate * grad_sum / row_rms
    return (gate_acc[None], up_acc[None], new_master[None])


def solution(mesh):
    return jax.shard_map(
        per_device,
        mesh=mesh,
        in_specs=(
            P("expert", "shard", None),
            P("expert", None, "shard"),
            P("expert", None, "shard"),
            P("expert", "shard"),
            P(),
            P("expert", "shard", None),
        ),
        out_specs=(
            P("expert", None, "shard"),
            P("expert", None, "shard"),
            P("expert", "shard", None),
        ),
        check_vma=False,
    )
```

profile of v0, /device:TPU:0, one launch (start us, length us, event | category | flops | bytes accessed | tf_op | source)
XLA Modules:
  0.0 284.9 jit_solution(8563610116932885319)
XLA Ops:
  7.2 0.0 all-gather.2.cloned.1.call-start
  7.9 2.1 bitcast_multiply_fusion
  10.0 0.0 all-gather.2.cloned.1.call-update
  10.0 0.0 copy-start.2
  10.0 94.5 %all-gather.2.cloned.1.call-done = bf16[2048,3072]{1,0:T(8,128)(2,1)} async-done(((bf16[128,3072]{1,0:T(8,128)(2,1)}), bf16[2048,3072]{1,0:T(8,128)(2,1)}) %all-gather.2.cloned.1.call-update) | async-done | bytes 12582928 | tf_op jit(solution)/shard_map/all_gather | solution.py:28
  104.5 13.4 %fusion.21 = (bf16[512,3072]{1,0:T(8,128)(2,1)}, f32[512,3072]{1,0:T(8,128)}) fusion(bf16[2048,3072]{1,0:T(8,128)(2,1)} %all-gather.2.cloned.1.call-done, bf16[1,2048,512]{2,1,0:T(8,128)(2,1)} %param.8, bf16[1,2048,512]{2,1,0:T(8,128)(2,1)} %param.7), kind=kOutput, calls=%fused_computation.36 | convolution fusion | flops 6452412416 | bytes 26214400 | tf_op jit(solution)/shard_map/dot_general | solution.py:34
  117.9 1.5 collective-permute-start
  119.4 0.0 copy-done.2
  119.4 0.7 fusion.18
  121.5 66.9 %collective-permute-done = bf16[512,3072]{1,0:T(8,128)(2,1)S(1)} collective-permute-done((bf16[512,3072]{1,0:T(8,128)(2,1)}, bf16[512,3072]{1,0:T(8,128)(2,1)S(1)}, u32[]{:S(2)}, u32[]{:S(2)}) %collective-permute-start) | collective-permute-done | bytes 3145760 | tf_op jit(solution)/shard_map/ppermute | solution.py:11
  188.4 0.0 copy-start
  188.4 1.6 copy-done
  190.1 0.0 slice-start
  190.1 6.6 %fusion.9 = bf16[512,3072]{1,0:T(8,128)(2,1)} fusion(f32[512,3072]{1,0:T(8,128)} %get-tuple-element.9, bf16[512,3072]{1,0:T(8,128)(2,1)} %copy-done, pred[]{:T(512)S(6)} %eq.28), kind=kLoop, calls=%fused_computation.20 | loop fusion | flops 6291456 | bytes 12582913 | tf_op jit(solution)/shard_map/convert_element_type | solution.py:39
  196.6 3.0 %collective-permute-start.1 = (bf16[512,3072]{1,0:T(8,128)(2,1)}, bf16[512,3072]{1,0:T(8,128)(2,1)}, u32[]{:S(2)}, u32[]{:S(2)}) collective-permute-start(bf16[512,3072]{1,0:T(8,128)(2,1)} %fusion.9), channel_id=1, source_target_pairs={{0,32},{16,48},{32,0},{48,16},{64,96},{80,112},{96,64},{112,80},{1... | collective-permute-start | bytes 9437192 | tf_op jit(solution)/shard_map/ppermute | solution.py:11
  200.9 0.0 slice-start.1
  200.9 0.0 copy-start.1
  200.9 16.6 %fusion.11 = (bf16[1,2048,512]{2,1,0:T(8,128)(2,1)}, bf16[1,2048,512]{2,1,0:T(8,128)(2,1)}) fusion(bf16[1,2048,512]{2,1,0:T(8,128)(2,1)} %param.7, bf16[1,2048,512]{2,1,0:T(8,128)(2,1)} %param.8, bf16[2048,3072]{1,0:T(8,128)(2,1)} %all-gather.2.cloned.1.call-done, f32[1,512,3072]{2,1,0:T(8,128)} %param.11), kind=kOutput, calls=%fused_computation.22 | convolution fusion | flops 6458179584 | bytes 27262976 | tf_op jit(solution)/shard_map/dot_general | solution.py:29
  217.5 50.4 %collective-permute-done.1 = bf16[512,3072]{1,0:T(8,128)(2,1)} collective-permute-done((bf16[512,3072]{1,0:T(8,128)(2,1)}, bf16[512,3072]{1,0:T(8,128)(2,1)}, u32[]{:S(2)}, u32[]{:S(2)}) %collective-permute-start.1) | collective-permute-done | bytes 3145760 | tf_op jit(solution)/shard_map/ppermute | solution.py:11
  267.9 0.0 slice-done
  267.9 0.0 slice-done.1
  267.9 0.0 copy-done.1
  267.9 3.6 %multiply_reduce_fusion = f32[512]{0:T(512)S(1)} fusion(bf16[512,3072]{1,0:T(8,128)(2,1)} %collective-permute-done.1, pred[]{:T(512)S(6)} %eq.31, f32[512,3072]{1,0:T(8,128)S(1)} %bitcast.54, bf16[512,3072]{1,0:T(8,128)(2,1)S(1)} %copy-done.1, pred[]{:T(512)S(6)} %eq.28), kind=kLoop, calls=%fused_computation.6 | loop fusion | flops 12582400 | bytes 12584962 | tf_op jit(solution)/shard_map/reduce_sum | solution.py:45
  271.6 6.5 %fusion = f32[1,512,3072]{2,1,0:T(8,128)} fusion(f32[1,512,3072]{2,1,0:T(8,128)} %param.11, f32[512]{0:T(512)S(1)} %add_sqrt_fusion, bf16[512,3072]{1,0:T(8,128)(2,1)} %collective-permute-done.1, pred[]{:T(512)S(6)} %eq.31, f32[512,3072]{1,0:T(8,128)S(1)} %bitcast.54, bf16[512,3072]{1,0:T(8,128)(2,1)S(1)} %copy-done.1, pred[]{:T(512)S(6)} %eq.28), kind=kLoop, calls=%fused_computation.5 | loop fusion | flops 14155776 | bytes 25167874 | tf_op jit(solution)/shard_map/broadcast_in_dim | solution.py:47
  (3 shorter events, 0.0 us)
Async XLA Ops:
  7.2 97.4 %all-gather.2.cloned.1.call-start = ((), (), s32[]{:S(2)}) async-start(), calls=%async_computation | async-start | bytes 13369344 | tf_op jit(solution)/shard_map/all_gather | solution.py:28
  10.0 109.4 %copy-start.2 = (s32[8]{0:T(128)S(1)}, s32[8]{0:T(128)}, u32[]{:S(2)}) copy-start(s32[8]{0:T(128)} %param.10) | copy-start | bytes 100
  117.9 70.5 %collective-permute-start = (bf16[512,3072]{1,0:T(8,128)(2,1)}, bf16[512,3072]{1,0:T(8,128)(2,1)S(1)}, u32[]{:S(2)}, u32[]{:S(2)}) collective-permute-start(bf16[512,3072]{1,0:T(8,128)(2,1)} %get-tuple-element.8), channel_id=1, source_target_pairs={{0,16},{16,0},{32,48},{48,32},{64,80},{80,64},{96,112},{112,96},{1... | collective-permute-start | bytes 9437192 | tf_op jit(solution)/shard_map/ppermute | solution.py:11
  188.4 1.6 copy-start
  190.1 77.8 %slice-start = ((s8[6291456]{0:T(1024)(128)(4,1)}), s8[2097152]{0:T(1024)(128)(4,1)S(1)}, s32[]{:S(2)}) async-start(s8[6291456]{0:T(1024)(128)(4,1)} %bitcast.53), calls=%async_computation.1 | async-start | bytes 4194304
  196.6 71.3 %collective-permute-start.1 = (bf16[512,3072]{1,0:T(8,128)(2,1)}, bf16[512,3072]{1,0:T(8,128)(2,1)}, u32[]{:S(2)}, u32[]{:S(2)}) collective-permute-start(bf16[512,3072]{1,0:T(8,128)(2,1)} %fusion.9), channel_id=1, source_target_pairs={{0,32},{16,48},{32,0},{48,16},{64,96},{80,112},{96,64},{112,80},{1... | collective-permute-start | bytes 9437192 | tf_op jit(solution)/shard_map/ppermute | solution.py:11
  200.9 67.0 %slice-start.1 = ((s8[6291456]{0:T(1024)(128)(4,1)}), s8[4194304]{0:T(1024)(128)(4,1)S(1)}, s32[]{:S(2)}) async-start(s8[6291456]{0:T(1024)(128)(4,1)} %bitcast.53), calls=%async_computation.2 | async-start | bytes 8388608
  200.9 67.0 %copy-start.1 = (bf16[512,3072]{1,0:T(8,128)(2,1)S(1)}, bf16[512,3072]{1,0:T(8,128)(2,1)}, u32[]{:S(2)}) copy-start(bf16[512,3072]{1,0:T(8,128)(2,1)} %copy-done) | copy-start | bytes 9437188
Sparse Core Ops, SparseCore 0:
  11.0 93.4 all-gather.1
where the time goes:
time: 285 us
  waiting for transfers between devices  212 us (74%)
  matrix products  30 us (11%)
  other arithmetic  19.6 us (7%)
  between operations  17.4 us (6%)
  starting transfers between devices  4.49 us (2%)
    ppermute x2, waiting for transfers between devices, from_partner(): lax.ppermute(shard, axis, [(i, i ^ 1 << bit) for i in range(lax.axis_size...  117 us
    all_gather x1, waiting for transfers between devices, per_device(): block_rows = lax.all_gather(masked, 'shard', axis=0, tiled=True)  94.5 us
    dot_general x1, matrix products, per_device(): lax.dot_general(block_rows, weight_work, (((1,), (1,)), ((), ())), prefer...  16.6 us
    dot_general x1, matrix products, per_device(): lax.dot_general(hidden, block_rows, (((0,), (0,)), ((), ())), preferred_e...  13.4 us
    convert_element_type x1, other arithmetic, per_device(): grad_sum.astype(jnp.bfloat16)  6.56 us
    broadcast_in_dim x1, other arithmetic, per_device(): return (gate_acc[None], up_acc[None], new_master[None])  6.48 us
  transfers between devices with their start and end apart: 3, of which 3 were waited for; matrix products, arithmetic and copies ran while one was open for 6% of the time, Pallas kernels for 0%

commit v1 on v0

--- a/solution.py
+++ b/solution.py
@@ -5,6 +5,13 @@
 
 learn_rate = 0.02
 rms_eps = 1e-06
+
+
+def _recover_records(z_in, a_name):
+    carry = jnp.concatenate(
+        lax.all_to_all(jnp.stack(lax.axis_size(a_name) * [z_in]), a_name, 0, 0), axis=0
+    )
+    return carry
 
 
 def from_partner(shard, axis, bit):
@@ -25,7 +32,7 @@
     my_slot = lax.axis_index("expert")
     slot_order = jnp.arange(placement.shape[0], dtype=jnp.int32)
     my_expert = jnp.sum(jnp.where(slot_order == my_slot, placement, 0))
-    block_rows = lax.all_gather(masked, "shard", axis=0, tiled=True)
+    block_rows = _recover_records(masked, "shard")
     d_hidden = lax.dot_general(
         block_rows, weight_work, (((1,), (1,)), ((), ())), preferred_element_type=jnp.float32
     )

time: 285 us -> 327 us (1.15)
  blocking collectives: 0 us -> 150 us
  waiting for transfers between devices: 212 us -> 115 us
  between operations: 17.4 us -> 3.98 us
  local copies, waits for them, and re-layouts: 1.67 us -> 7.88 us
  matrix products: 30 us -> 26.3 us
    all_to_all x0 -> x1, blocking collectives: none -> 150 us  [_recover_records(): lax.all_to_all(jnp.stack(lax.axis_size(a_name) * [z_in]), a_name, 0, 0)]
    all_gather x1 -> x0, waiting for transfers between devices: 94.5 us -> none  [per_device(): block_rows = lax.all_gather(masked, 'shard', axis=0, tiled=True)]
    another operation x0 -> x1, local copies, waits for them, and re-layouts: none -> 6.21 us  [_recover_records(): jnp.stack(lax.axis_size(a_name) * [z_in])]
    dot_general x1, matrix products: 13.4 us -> 9.65 us  [per_device(): lax.dot_general(hidden, block_rows, (((0,), (0,)), ((), ())), preferred_e...]
  transfers between devices with their start and end apart: 3 -> 2, of which waited for: 3 -> 2; matrix products, arithmetic and copies ran while one was open for 6% -> 5% of each run, Pallas kernels for 0% -> 0%
where the time goes in v1:
time: 327 us
  blocking collectives  150 us (46%)
  waiting for transfers between devices  115 us (35%)
  matrix products  26.3 us (8%)
  other arithmetic  18.7 us (6%)
  local copies, waits for them, and re-layouts  7.88 us (2%)
  starting transfers between devices  4.51 us (1%)
  between operations  3.98 us (1%)
    all_to_all x1, blocking collectives, _recover_records(): lax.all_to_all(jnp.stack(lax.axis_size(a_name) * [z_in]), a_name, 0, 0)  150 us
    ppermute x2, waiting for transfers between devices, from_partner(): lax.ppermute(shard, axis, [(i, i ^ 1 << bit) for i in range(lax.axis_size...  115 us
    dot_general x1, matrix products, per_device(): lax.dot_general(block_rows, weight_work, (((1,), (1,)), ((), ())), prefer...  16.6 us
    dot_general x1, matrix products, per_device(): lax.dot_general(hidden, block_rows, (((0,), (0,)), ((), ())), preferred_e...  9.65 us
    convert_element_type x1, other arithmetic, per_device(): grad_sum.astype(jnp.bfloat16)  6.56 us
  transfers between devices with their start and end apart: 2, of which 2 were waited for; matrix products, arithmetic and copies ran while one was open for 5% of the time, Pallas kernels for 0%

profile of v1, /device:TPU:0, one launch (start us, length us, event | category | flops | bytes accessed | tf_op | source)
XLA Modules:
  0.0 326.6 jit_solution(9414034670711462292)
XLA Ops:
  1.3 1.3 multiply_bitcast_fusion
  2.5 6.2 %stack.5 = bf16[16,128,3072]{2,1,0:T(8,128)(2,1)} broadcast(bf16[128,3072]{1,0:T(8,128)(2,1)S(1)} %multiply_bitcast_fusion), dimensions={1,2} | broadcast | bytes 13369344 | tf_op jit(solution)/shard_map/stack | solution.py:12
  8.8 0.0 copy-start.4
  8.8 0.0 copy-start.5
  8.8 149.8 %all_to_all.5 = bf16[16,128,3072]{2,1,0:T(8,128)(2,1)S(1)} all-to-all(bf16[16,128,3072]{2,1,0:T(8,128)(2,1)} %stack.5), channel_id=1, replica_groups=mesh['expert'=8,'shard'=16] {'shard'}, dimensions={0} | all-to-all | bytes 25165824 | tf_op jit(solution)/shard_map/all_to_all | solution.py:12
  158.6 0.0 copy-start.2
  158.6 0.0 copy-done.4
  158.6 0.0 copy-done.5
  158.6 0.0 copy-start.3
  158.6 9.6 %fusion.31 = (bf16[512,3072]{1,0:T(8,128)(2,1)}, f32[512,3072]{1,0:T(8,128)}) fusion(bf16[2048,3072]{1,0:T(8,128)(2,1)S(1)} %bitcast.71, bf16[1,2048,512]{2,1,0:T(8,128)(2,1)S(1)} %copy-done.5, bf16[1,2048,512]{2,1,0:T(8,128)(2,1)S(1)} %copy-done.4), kind=kOutput, calls=%fused_computation.45 | convolution fusion | flops 6452412416 | bytes 26214400 | tf_op jit(solution)/shard_map/dot_general | solution.py:41
  168.2 0.0 copy-done.2
  168.2 1.5 collective-permute-start
  169.7 0.0 copy-done.3
  169.7 0.7 fusion.29
  171.8 66.1 %collective-permute-done = bf16[512,3072]{1,0:T(8,128)(2,1)S(1)} collective-permute-done((bf16[512,3072]{1,0:T(8,128)(2,1)}, bf16[512,3072]{1,0:T(8,128)(2,1)S(1)}, u32[]{:S(2)}, u32[]{:S(2)}) %collective-permute-start) | collective-permute-done | bytes 3145760 | tf_op jit(solution)/shard_map/ppermute | solution.py:18
  237.9 0.0 copy-start
  237.9 1.6 copy-done
  239.5 0.0 slice-start
  239.5 6.6 %fusion.18 = bf16[512,3072]{1,0:T(8,128)(2,1)} fusion(f32[512,3072]{1,0:T(8,128)} %get-tuple-element.9, bf16[512,3072]{1,0:T(8,128)(2,1)} %copy-done, pred[]{:T(512)S(6)} %eq.28), kind=kLoop, calls=%fused_computation.27 | loop fusion | flops 6291456 | bytes 12582913 | tf_op jit(solution)/shard_map/convert_element_type | solution.py:46
  246.1 3.0 collective-permute-start.1
  250.4 0.0 slice-start.1
  250.4 0.0 copy-start.1
  250.4 16.6 %fusion.25 = (bf16[1,2048,512]{2,1,0:T(8,128)(2,1)}, bf16[1,2048,512]{2,1,0:T(8,128)(2,1)}) fusion(bf16[1,2048,512]{2,1,0:T(8,128)(2,1)} %param.7, bf16[1,2048,512]{2,1,0:T(8,128)(2,1)} %param.8, bf16[2048,3072]{1,0:T(8,128)(2,1)} %bitcast.72, f32[1,512,3072]{2,1,0:T(8,128)} %param.11), kind=kOutput, calls=%fused_computation.33 | convolution fusion | flops 6459752448 | bytes 27262976 | tf_op jit(solution)/shard_map/dot_general | solution.py:36
  267.1 49.4 %collective-permute-done.1 = bf16[512,3072]{1,0:T(8,128)(2,1)} collective-permute-done((bf16[512,3072]{1,0:T(8,128)(2,1)}, bf16[512,3072]{1,0:T(8,128)(2,1)}, u32[]{:S(2)}, u32[]{:S(2)}) %collective-permute-start.1) | collective-permute-done | bytes 3145760 | tf_op jit(solution)/shard_map/ppermute | solution.py:18
  316.4 0.0 slice-done
  316.4 0.0 slice-done.1
  316.4 0.0 copy-done.1
  316.4 3.6 %multiply_reduce_fusion = f32[512]{0:T(512)S(1)} fusion(bf16[512,3072]{1,0:T(8,128)(2,1)} %collective-permute-done.1, pred[]{:T(512)S(6)} %eq.31, f32[512,3072]{1,0:T(8,128)S(1)} %bitcast.70, bf16[512,3072]{1,0:T(8,128)(2,1)S(1)} %copy-done.1, pred[]{:T(512)S(6)} %eq.28), kind=kLoop, calls=%fused_computation.8 | loop fusion | flops 12582400 | bytes 12584962 | tf_op jit(solution)/shard_map/reduce_sum | solution.py:52
  320.1 6.5 %fusion = f32[1,512,3072]{2,1,0:T(8,128)} fusion(f32[1,512,3072]{2,1,0:T(8,128)} %param.11, f32[512]{0:T(512)S(1)} %add_sqrt_fusion, bf16[512,3072]{1,0:T(8,128)(2,1)} %collective-permute-done.1, pred[]{:T(512)S(6)} %eq.31, f32[512,3072]{1,0:T(8,128)S(1)} %bitcast.70, bf16[512,3072]{1,0:T(8,128)(2,1)S(1)} %copy-done.1, pred[]{:T(512)S(6)} %eq.28), kind=kLoop, calls=%fused_computation.1 | loop fusion | flops 14155776 | bytes 25167874 | tf_op jit(solution)/shard_map/broadcast_in_dim | solution.py:54
  (3 shorter events, 0.0 us)
Async XLA Ops:
  8.8 149.8 %copy-start.4 = (bf16[1,2048,512]{2,1,0:T(8,128)(2,1)S(1)}, bf16[1,2048,512]{2,1,0:T(8,128)(2,1)}, u32[]{:S(2)}) copy-start(bf16[1,2048,512]{2,1,0:T(8,128)(2,1)} %param.7) | copy-start | bytes 6291460
  8.8 149.8 %copy-start.5 = (bf16[1,2048,512]{2,1,0:T(8,128)(2,1)S(1)}, bf16[1,2048,512]{2,1,0:T(8,128)(2,1)}, u32[]{:S(2)}) copy-start(bf16[1,2048,512]{2,1,0:T(8,128)(2,1)} %param.8) | copy-start | bytes 6291460
  158.6 9.7 %copy-start.2 = (bf16[16,128,3072]{2,1,0:T(8,128)(2,1)}, bf16[16,128,3072]{2,1,0:T(8,128)(2,1)S(1)}, u32[]{:S(2)}) copy-start(bf16[16,128,3072]{2,1,0:T(8,128)(2,1)S(1)} %all_to_all.5) | copy-start | bytes 37748740
  158.6 11.2 %copy-start.3 = (s32[8]{0:T(128)S(1)}, s32[8]{0:T(128)}, u32[]{:S(2)}) copy-start(s32[8]{0:T(128)} %param.10) | copy-start | bytes 100
  168.2 69.6 %collective-permute-start = (bf16[512,3072]{1,0:T(8,128)(2,1)}, bf16[512,3072]{1,0:T(8,128)(2,1)S(1)}, u32[]{:S(2)}, u32[]{:S(2)}) collective-permute-start(bf16[512,3072]{1,0:T(8,128)(2,1)} %get-tuple-element.8), channel_id=1, source_target_pairs={{0,16},{16,0},{32,48},{48,32},{64,80},{80,64},{96,112},{112,96},{1... | collective-permute-start | bytes 9437192 | tf_op jit(solution)/shard_map/ppermute | solution.py:18
  237.9 1.6 copy-start
  239.5 76.9 %slice-start = ((s8[6291456]{0:T(1024)(128)(4,1)}), s8[2097152]{0:T(1024)(128)(4,1)S(1)}, s32[]{:S(2)}) async-start(s8[6291456]{0:T(1024)(128)(4,1)} %bitcast.69), calls=%async_computation.1 | async-start | bytes 4194304
  246.1 70.3 %collective-permute-start.1 = (bf16[512,3072]{1,0:T(8,128)(2,1)}, bf16[512,3072]{1,0:T(8,128)(2,1)}, u32[]{:S(2)}, u32[]{:S(2)}) collective-permute-start(bf16[512,3072]{1,0:T(8,128)(2,1)} %fusion.18), channel_id=1, source_target_pairs={{0,32},{16,48},{32,0},{48,16},{64,96},{80,112},{96,64},{112,80},{1... | collective-permute-start | bytes 9437192 | tf_op jit(solution)/shard_map/ppermute | solution.py:18
  250.4 66.0 %slice-start.1 = ((s8[6291456]{0:T(1024)(128)(4,1)}), s8[4194304]{0:T(1024)(128)(4,1)S(1)}, s32[]{:S(2)}) async-start(s8[6291456]{0:T(1024)(128)(4,1)} %bitcast.69), calls=%async_computation.2 | async-start | bytes 8388608
  250.4 66.0 %copy-start.1 = (bf16[512,3072]{1,0:T(8,128)(2,1)S(1)}, bf16[512,3072]{1,0:T(8,128)(2,1)}, u32[]{:S(2)}) copy-start(bf16[512,3072]{1,0:T(8,128)(2,1)} %copy-done) | copy-start | bytes 9437188
